TPU v7x, 512 devices: a whole 4x8x8 slice. The times are simulated.
512 devices in a mesh: img: 16 (over x, y_lo, core), vol: 32 (over z, y_hi).
Axes of the slice: x: 4, y: 8 (y_hi: 4, y_lo: 2; y = y_hi * 2 + y_lo), z: 8, core: 2. Of those that a mesh axis runs over, the one named last changes fastest.
Arguments:
- volume: float32 [512, 16, 4, 256], P('vol', 'img'), may hold values from -6 to 6
- images: bfloat16 [16384, 8, 256], P(('img', 'vol')), may hold values from -6 to 6
- ctf: float32 [16384, 8, 128], P(('img', 'vol')), may hold values from -1 to 1
- noise_weight: float32 [16384, 8, 128], P(('img', 'vol')), may hold values from 0.025 to 8, as said below
- shifts: float32 [16384, 2, 32], P(('img', 'vol')), may hold values from -4 to 4
- orient: int32 [16384, 64], P(('img', 'vol')), may hold values from 0 to 191, all different within a row
- counts: int32 [16384], P(('img', 'vol')), may hold values from 1 to 64
- tile_map: int32 [192, 8, 8], replicated, may hold values from 0 to 32767
- interp: float32 [192, 8, 8], replicated, may hold values from 0.05 to 0.3
Outputs:
- real_space: float32 [2, 512, 16, 512], P(None, None, 'img', 'vol')
- evidence: float32 [16384], P(('img', 'vol'))
Inputs may be any that keep to these rules, and one draw needn't show every extreme that they name: `orient`: the 64 entries of one image are different orientations. `noise_weight`: positive.
All inputs are finite; a program needn't handle non-finite values.
Results may differ from a plain program's by a relative error of at most 0.0068.
Values may be sent and summed in bfloat16 or wider, within the bound.
No kernel may reach another device: no remote copies, remote signals or barrier semaphores. Data moves between devices by JAX's collectives and lax.ppermute only.
A program may use at most 64 MiB of HBM per device.

v0:
```python
import math
import jax
import jax.numpy as jnp
from jax import lax
from jax.sharding import PartitionSpec as P

BOX = 256
precise = lax.Precision.HIGHEST


def shifted_weighted(images, ctf, noise_weight, shifts):
    num_images, rows_per, width = images.shape
    tile_len = width // 2
    row_freq = jnp.arange(rows_per, dtype=jnp.float32) / BOX
    col_freq = jnp.arange(tile_len, dtype=jnp.float32) / BOX
    angle = (
        -2.0
        * math.pi
        * (
            shifts[:, 0, :, None, None] * col_freq[None, None, None, :]
            + shifts[:, 1, :, None, None] * row_freq[None, None, :, None]
        )
    )
    cosine = jnp.cos(angle)
    sine = jnp.sin(angle)
    real_part = images[:, None, :, :tile_len].astype(jnp.float32)
    imag_part = images[:, None, :, tile_len:].astype(jnp.float32)
    factor = (noise_weight * ctf)[:, None]
    moved_re = (real_part * cosine - imag_part * sine) * factor
    moved_im = (real_part * sine + imag_part * cosine) * factor
    joined = jnp.concatenate([moved_re, moved_im], axis=-1).astype(jnp.bfloat16)
    return joined.reshape(num_images * shifts.shape[2], rows_per * width)


def score_block(weighted, slice_mat, power, ctf, noise_weight, orient, counts, trials):
    num_images = ctf.shape[0]
    orients = slice_mat.shape[0]
    slots = orient.shape[1]
    cross = lax.dot_general(
        weighted, slice_mat, (((1,), (1,)), ((), ())), preferred_element_type=jnp.float32
    )
    cross = cross.reshape(num_images, trials, orients)
    squared = (noise_weight * ctf * ctf).reshape(num_images, -1)
    penalty = jnp.dot(0.5 * squared, power.T, precision=precise)
    score = cross - penalty[:, None, :]
    onehot = (orient[:, :, None] == jnp.arange(orients, dtype=jnp.int32)[None, None, :]).astype(
        jnp.float32
    )
    picked = jnp.einsum("ito,ijo->ijt", score, onehot, precision=precise)
    usable = jnp.arange(slots, dtype=jnp.int32)[None, :] < counts[:, None]
    logits = jnp.where(usable[:, :, None], picked, -jnp.inf)
    highest = jnp.max(logits, axis=(1, 2))
    expo = jnp.exp(logits - highest[:, None, None])
    total = jnp.sum(expo, axis=(1, 2))
    evidence = highest + jnp.log(total)
    gamma = expo / total[:, None, None]
    spread = jnp.einsum("ijt,ijo->ito", gamma, onehot, precision=precise)
    spread_low = spread.astype(jnp.bfloat16).reshape(num_images * trials, orients)
    back_data = lax.dot_general(
        spread_low, weighted, (((0,), (0,)), ((), ())), preferred_element_type=jnp.float32
    )
    back_weight = jnp.dot(jnp.sum(spread, axis=1).T, squared, precision=precise)
    return (back_data, back_weight, evidence)


def spread_tiles(data_rows, weight_rows, chosen, target_row, interp, capacity):
    acc_data = jnp.zeros((capacity, data_rows.shape[1]), jnp.float32)
    acc_weight = jnp.zeros((capacity, weight_rows.shape[1]), jnp.float32)
    for term_index in range(interp.shape[2]):
        target = jnp.where(
            chosen[:, :, term_index], target_row[:, :, term_index], capacity
        ).reshape(-1)
        scaled = interp[:, :, term_index].reshape(-1, 1)
        acc_data = acc_data.at[target].add(scaled * data_rows, mode="drop")
        acc_weight = acc_weight.at[target].add(scaled * weight_rows, mode="drop")
    return (acc_data, acc_weight)


def dft_tables(length):
    steps = jnp.arange(length, dtype=jnp.int32)
    product = steps[:, None] * steps[None, :] % length
    angle = product.astype(jnp.float32) * (2.0 * math.pi / length)
    norming = 1.0 / math.sqrt(length)
    return (jnp.cos(angle) * norming, jnp.sin(angle) * norming)


def centred_sinc(positions, length):
    centred = ((positions + length // 2) % length - length // 2).astype(jnp.float32) / length
    return jnp.sinc(centred) ** 2


def on_device(volume, images, ctf, noise_weight, shifts, orient, counts, tile_map, interp):
    vol_count = lax.axis_size("vol")
    img_count = lax.axis_size("img")
    vol_index = lax.axis_index("vol")
    img_index = lax.axis_index("img")
    slab_depth, planes_dev, per_line, width = volume.shape
    tile_len = width // 2
    planes_all = planes_dev * img_count
    depth_len = slab_depth * vol_count
    line_len = per_line * tile_len
    orients, rows_per, terms = tile_map.shape
    trials = shifts.shape[2]
    flat_tiles = volume.reshape(slab_depth * planes_dev * per_line, width)
    tile_depth = tile_map // (planes_all * per_line)
    tile_plane = tile_map // per_line % planes_all
    tile_quarter = tile_map % per_line
    on_slab = tile_depth // slab_depth == vol_index
    owned = on_slab & (tile_plane // planes_dev == img_index)
    local_row = (
        (tile_depth - vol_index * slab_depth) * planes_dev + (tile_plane - img_index * planes_dev)
    ) * per_line + tile_quarter
    partial_value = jnp.zeros((orients, rows_per, width), jnp.float32)
    for term_index in range(terms):
        factor = jnp.where(owned[:, :, term_index], interp[:, :, term_index], 0.0)
        fetched = jnp.take(
            flat_tiles, jnp.where(owned[:, :, term_index], local_row[:, :, term_index], 0), axis=0
        )
        partial_value = partial_value + factor[:, :, None] * fetched
    partial_value = partial_value.reshape(orients * rows_per, width)
    slices = lax.psum(partial_value, ("img", "vol")).astype(jnp.bfloat16)
    slice_mat = slices.reshape(orients, rows_per * width)
    widened = slices.astype(jnp.float32).reshape(orients, rows_per, width)
    power = (widened[:, :, :tile_len] ** 2 + widened[:, :, tile_len:] ** 2).reshape(
        orients, rows_per * tile_len
    )
    num_images = images.shape[0]
    block_len = min(16, num_images)
    blocks = num_images // block_len

    def one_block(carry, block):
        weighted = shifted_weighted(block[0], block[1], block[2], block[3])
        back_data, back_weight, evidence = score_block(
            weighted, slice_mat, power, block[1], block[2], block[4], block[5], trials
        )
        return ((carry[0] + back_data, carry[1] + back_weight), evidence)

    start = (
        jnp.zeros((orients, rows_per * width), jnp.float32),
        jnp.zeros((orients, rows_per * tile_len), jnp.float32),
    )
    inputs = (
        images.reshape(blocks, block_len, rows_per, width),
        ctf.reshape(blocks, block_len, rows_per, tile_len),
        noise_weight.reshape(blocks, block_len, rows_per, tile_len),
        shifts.reshape(blocks, block_len, 2, trials),
        orient.reshape(blocks, block_len, orient.shape[1]),
        counts.reshape(blocks, block_len),
    )
    (back_data, back_weight), evidence = lax.scan(one_block, start, inputs)
    data_rows = back_data.reshape(orients * rows_per, width)
    weight_rows = back_weight.reshape(orients * rows_per, tile_len)
    data_rows, weight_rows = lax.psum((data_rows, weight_rows), ("img", "vol"))
    acc_data, acc_weight = spread_tiles(
        data_rows, weight_rows, owned, local_row, interp, slab_depth * planes_dev * per_line
    )
    acc_data = acc_data.reshape(slab_depth, planes_dev, per_line, width)
    denominator = acc_weight.reshape(slab_depth, planes_dev, line_len) + 1.0
    field_re = acc_data[:, :, :, :tile_len].reshape(slab_depth, planes_dev, line_len) / denominator
    field_im = acc_data[:, :, :, tile_len:].reshape(slab_depth, planes_dev, line_len) / denominator
    cos_line, sin_line = dft_tables(line_len)
    lines_re = jnp.einsum("zxk,kn->zxn", field_re, cos_line, precision=precise) - jnp.einsum(
        "zxk,kn->zxn", field_im, sin_line, precision=precise
    )
    lines_im = jnp.einsum("zxk,kn->zxn", field_re, sin_line, precision=precise) + jnp.einsum(
        "zxk,kn->zxn", field_im, cos_line, precision=precise
    )
    stacked = jnp.stack([lines_re, lines_im])
    columns = lax.all_to_all(stacked, "vol", split_axis=3, concat_axis=1, tiled=True)
    cos_depth, sin_depth = dft_tables(depth_len)
    out_re = jnp.einsum("nk,kxy->nxy", cos_depth, columns[0], precision=precise) - jnp.einsum(
        "nk,kxy->nxy", sin_depth, columns[1], precision=precise
    )
    out_im = jnp.einsum("nk,kxy->nxy", sin_depth, columns[0], precision=precise) + jnp.einsum(
        "nk,kxy->nxy", cos_depth, columns[1], precision=precise
    )
    y_block = columns.shape[3]
    depth_corr = centred_sinc(jnp.arange(depth_len, dtype=jnp.int32), depth_len)
    line_corr = centred_sinc(vol_index * y_block + jnp.arange(y_block, dtype=jnp.int32), line_len)
    correction = depth_corr[:, None, None] * line_corr[None, None, :]
    real_space = jnp.stack([out_re / correction, out_im / correction])
    return (real_space, evidence.reshape(num_images))


def solution(mesh):
    placed = (
        P("vol", "img", None, None),
        P(("img", "vol"), None, None),
        P(("img", "vol"), None, None),
        P(("img", "vol"), None, None),
        P(("img", "vol"), None, None),
        P(("img", "vol"), None),
        P(("img", "vol")),
        P(),
        P(),
    )
    return jax.shard_map(
        on_device,
        mesh=mesh,
        in_specs=placed,
        out_specs=(P(None, None, "img", "vol"), P(("img", "vol"))),
        check_vma=False,
    )
```

profile of v0, /device:TPU:1, one launch (start us, length us, event | category | flops | bytes accessed | tf_op | source)
XLA Modules:
  0.0 750.6 jit_solution(8383923017051528959)
XLA Ops:
  29.7 4.7 gather_fusion.5
  39.5 4.7 gather_fusion.7
  49.3 4.7 gather_fusion.1
  55.9 10.9 %fusion.17 = f32[1536,256]{1,0:T(8,128)} fusion(f32[1536,256]{1,0:T(8,128)} %gather_fusion.7, f32[1536,256]{1,0:T(8,128)} %gather_fusion.6, f32[1536,256]{1,0:T(8,128)} %gather_fusion.5, f32[1536,256]{1,0:T(8,128)} %gather_fusion.4, f32[1536,256]{1,0:T(8,128)S(1)} %gather_fusion.3, f32[1536,256]{1,0:T(8,128)S(1)} %gather_fusion.2, ...), kind=kLoop, calls=%fused_computation.71 | loop fusion | flops 9043968 | bytes 14217216 | tf_op jit(solution)/shard_map/reshape | solution.py:120
  66.8 112.6 %all-reduce.5 = bf16[1536,256]{1,0:T(8,128)(2,1)S(1)} all-reduce(f32[1536,256]{1,0:T(8,128)} %fusion.17), channel_id=1, replica_groups=mesh['img'=16,'vol'=32] {'img','vol'}, use_global_device_ids=true, to_apply=%region_0.2 | all-reduce | flops 393216 | bytes 2359296 | tf_op jit(solution)/shard_map/psum | solution.py:121
  181.5 58.8 %while.15 = (s32[]{:T(128)}, f32[192,2048]{1,0:T(8,128)}, f32[192,1024]{1,0:T(8,128)}, f32[2,16]{1,0:T(2,128)}, s32[2,16]{1,0:T(2,128)S(1)}, /*index=5*/s32[2,16...) while((s32[]{:T(128)}, f32[192,2048]{1,0:T(8,128)}, ...), condition=%wide.region_5.7_spmd.clone, body=%wide.region_1.6_spmd.clone.sunk | while | flops 1044547712 | bytes 34849968 | solution.py:150
  184.3 8.7 %subtract_multiply_fusion.2 = (bf16[16,32,8,128]{3,2,1,0:T(8,128)(2,1)S(1)}, bf16[16,32,8,128]{3,2,1,0:T(8,128)(2,1)S(1)}) fusion(f32[16,8,128]{2,1,0:T(8,128)S(1)} %get-tuple-element.305, f32[16,8,128]{2,1,0:T(8,128)S(1)} %get-tuple-element.306, f32[16,32,8]{2,1,0:T(8,128)S(1)} %broadcast_multiply_fusion.4, ...), kind=kLoop, calls=%fused_computation.27.clone.1 | loop fusion | flops 6291456 | bytes 2572288 | tf_op jit(solution)/shard_map/while/body/eval_jaxpr/mul | solution.py:29
  213.5 8.7 %subtract_multiply_fusion.2 = (bf16[16,32,8,128]{3,2,1,0:T(8,128)(2,1)S(1)}, bf16[16,32,8,128]{3,2,1,0:T(8,128)(2,1)S(1)}) fusion(f32[16,8,128]{2,1,0:T(8,128)S(1)} %get-tuple-element.305, f32[16,8,128]{2,1,0:T(8,128)S(1)} %get-tuple-element.306, f32[16,32,8]{2,1,0:T(8,128)S(1)} %broadcast_multiply_fusion.4, ...), kind=kLoop, calls=%fused_computation.27.clone.1 | loop fusion | flops 6291456 | bytes 2572288 | tf_op jit(solution)/shard_map/while/body/eval_jaxpr/mul | solution.py:29
  248.6 271.2 %all-reduce.4.cloned.1.call-done = (f32[1536,128]{1,0:T(8,128)}, f32[1536,256]{1,0:T(8,128)}) async-done(((f32[1536,128]{1,0:T(8,128)}, f32[1536,256]{1,0:T(8,128)}), (f32[1536,128]{1,0:T(8,128)}, f32[1536,256]{1,0:T(8,128)})) %all-reduce.4.cloned.1.call-update) | async-done | bytes 2359312 | tf_op jit(solution)/shard_map/psum | solution.py:153
  519.8 10.4 %scatter_custom_fusion = f32[64,256]{1,0:T(8,128)S(1)} fusion(s32[1536]{0:T(1024)S(1)} %fusion.130, f32[1536,256]{1,0:T(8,128)} %get-tuple-element.146, f32[1536]{0:T(1024)S(1)} %mul.631, f32[]{:T(128)} %constant.215.clone.1), kind=kCustom, calls=%fused_computation.106 | custom fusion | flops 786432 | bytes 1646596 | tf_op jit(solution)/shard_map/scatter-add | solution.py:74
  530.2 9.6 %scatter_custom_fusion.1 = f32[64,256]{1,0:T(8,128)S(1)} fusion(f32[64,256]{1,0:T(8,128)S(1)} %scatter_custom_fusion, s32[1536]{0:T(1024)S(1)} %fusion.131, f32[1536,256]{1,0:T(8,128)S(1)} %copy-done, f32[1536]{0:T(1024)S(1)} %mul.658), kind=kCustom, calls=%fused_computation.104 | custom fusion | flops 786432 | bytes 1646592 | tf_op jit(solution)/shard_map/scatter-add | solution.py:74
  539.8 9.6 %scatter_custom_fusion.2 = f32[64,256]{1,0:T(8,128)S(1)} fusion(f32[64,256]{1,0:T(8,128)S(1)} %scatter_custom_fusion.1, s32[1536]{0:T(1024)S(1)} %fusion.132, f32[1536,256]{1,0:T(8,128)S(1)} %copy-done, f32[1536]{0:T(1024)S(1)} %mul.661), kind=kCustom, calls=%fused_computation.102 | custom fusion | flops 786432 | bytes 1646592 | tf_op jit(solution)/shard_map/scatter-add | solution.py:74
  549.5 9.6 %scatter_custom_fusion.3 = f32[64,256]{1,0:T(8,128)S(1)} fusion(f32[64,256]{1,0:T(8,128)S(1)} %scatter_custom_fusion.2, s32[1536]{0:T(1024)S(1)} %fusion.133, f32[1536,256]{1,0:T(8,128)S(1)} %copy-done, f32[1536]{0:T(1024)S(1)} %mul.664), kind=kCustom, calls=%fused_computation.100 | custom fusion | flops 786432 | bytes 1646592 | tf_op jit(solution)/shard_map/scatter-add | solution.py:74
  559.1 10.1 %scatter_custom_fusion.4 = f32[64,256]{1,0:T(8,128)S(1)} fusion(f32[64,256]{1,0:T(8,128)S(1)} %scatter_custom_fusion.3, s32[1536]{0:T(1024)S(1)} %fusion.134, f32[1536,256]{1,0:T(8,128)S(1)} %copy-done, f32[1536]{0:T(1024)S(1)} %mul.667), kind=kCustom, calls=%fused_computation.98 | custom fusion | flops 786432 | bytes 1646592 | tf_op jit(solution)/shard_map/scatter-add | solution.py:74
  569.1 9.6 %scatter_custom_fusion.5 = f32[64,256]{1,0:T(8,128)S(1)} fusion(f32[64,256]{1,0:T(8,128)S(1)} %scatter_custom_fusion.4, s32[1536]{0:T(1024)S(1)} %fusion.135, f32[1536,256]{1,0:T(8,128)S(1)} %copy-done, f32[1536]{0:T(1024)S(1)} %mul.670), kind=kCustom, calls=%fused_computation.96 | custom fusion | flops 786432 | bytes 1646592 | tf_op jit(solution)/shard_map/scatter-add | solution.py:74
  578.8 9.6 %scatter_custom_fusion.6 = f32[64,256]{1,0:T(8,128)S(1)} fusion(f32[64,256]{1,0:T(8,128)S(1)} %scatter_custom_fusion.5, s32[1536]{0:T(1024)S(1)} %fusion.136, f32[1536,256]{1,0:T(8,128)S(1)} %copy-done, f32[1536]{0:T(1024)S(1)} %mul.673), kind=kCustom, calls=%fused_computation.94 | custom fusion | flops 786432 | bytes 1646592 | tf_op jit(solution)/shard_map/scatter-add | solution.py:74
  588.4 9.6 %scatter_custom_fusion.7 = f32[64,256]{1,0:T(8,128)S(1)} fusion(f32[64,256]{1,0:T(8,128)S(1)} %scatter_custom_fusion.6, s32[1536]{0:T(1024)S(1)} %fusion.137, f32[1536,256]{1,0:T(8,128)S(1)} %copy-done, f32[1536]{0:T(1024)S(1)} %mul.676), kind=kCustom, calls=%fused_computation.92 | custom fusion | flops 786432 | bytes 1646592 | tf_op jit(solution)/shard_map/scatter-add | solution.py:74
  598.1 9.7 %scatter_custom_fusion.8 = f32[64,128]{1,0:T(8,128)S(1)} fusion(s32[1536]{0:T(1024)S(1)} %fusion.130, f32[1536,128]{1,0:T(8,128)S(1)} %copy-done.1, f32[1536]{0:T(1024)S(1)} %mul.631, f32[]{:T(128)} %constant.229.clone.1), kind=kCustom, calls=%fused_computation.148 | custom fusion | flops 393216 | bytes 827396 | tf_op jit(solution)/shard_map/scatter-add | solution.py:75
  607.8 9.6 %scatter_custom_fusion.9 = f32[64,128]{1,0:T(8,128)S(1)} fusion(f32[64,128]{1,0:T(8,128)S(1)} %scatter_custom_fusion.8, s32[1536]{0:T(1024)S(1)} %fusion.131, f32[1536,128]{1,0:T(8,128)S(1)} %copy-done.1, f32[1536]{0:T(1024)S(1)} %mul.658), kind=kCustom, calls=%fused_computation.146 | custom fusion | flops 393216 | bytes 827392 | tf_op jit(solution)/shard_map/scatter-add | solution.py:75
  617.4 9.6 %scatter_custom_fusion.10 = f32[64,128]{1,0:T(8,128)S(1)} fusion(f32[64,128]{1,0:T(8,128)S(1)} %scatter_custom_fusion.9, s32[1536]{0:T(1024)S(1)} %fusion.132, f32[1536,128]{1,0:T(8,128)S(1)} %copy-done.1, f32[1536]{0:T(1024)S(1)} %mul.661), kind=kCustom, calls=%fused_computation.144 | custom fusion | flops 393216 | bytes 827392 | tf_op jit(solution)/shard_map/scatter-add | solution.py:75
  626.9 9.6 %scatter_custom_fusion.11 = f32[64,128]{1,0:T(8,128)S(1)} fusion(f32[64,128]{1,0:T(8,128)S(1)} %scatter_custom_fusion.10, s32[1536]{0:T(1024)S(1)} %fusion.133, f32[1536,128]{1,0:T(8,128)S(1)} %copy-done.1, f32[1536]{0:T(1024)S(1)} %mul.664), kind=kCustom, calls=%fused_computation.142 | custom fusion | flops 393216 | bytes 827392 | tf_op jit(solution)/shard_map/scatter-add | solution.py:75
  636.5 9.6 %scatter_custom_fusion.12 = f32[64,128]{1,0:T(8,128)S(1)} fusion(f32[64,128]{1,0:T(8,128)S(1)} %scatter_custom_fusion.11, s32[1536]{0:T(1024)S(1)} %fusion.134, f32[1536,128]{1,0:T(8,128)S(1)} %copy-done.1, f32[1536]{0:T(1024)S(1)} %mul.667), kind=kCustom, calls=%fused_computation.140 | custom fusion | flops 393216 | bytes 827392 | tf_op jit(solution)/shard_map/scatter-add | solution.py:75
  646.1 9.6 %scatter_custom_fusion.13 = f32[64,128]{1,0:T(8,128)S(1)} fusion(f32[64,128]{1,0:T(8,128)S(1)} %scatter_custom_fusion.12, s32[1536]{0:T(1024)S(1)} %fusion.135, f32[1536,128]{1,0:T(8,128)S(1)} %copy-done.1, f32[1536]{0:T(1024)S(1)} %mul.670), kind=kCustom, calls=%fused_computation.138 | custom fusion | flops 393216 | bytes 827392 | tf_op jit(solution)/shard_map/scatter-add | solution.py:75
  655.7 9.6 %scatter_custom_fusion.14 = f32[64,128]{1,0:T(8,128)S(1)} fusion(f32[64,128]{1,0:T(8,128)S(1)} %scatter_custom_fusion.13, s32[1536]{0:T(1024)S(1)} %fusion.136, f32[1536,128]{1,0:T(8,128)S(1)} %copy-done.1, f32[1536]{0:T(1024)S(1)} %mul.673), kind=kCustom, calls=%fused_computation.136 | custom fusion | flops 393216 | bytes 827392 | tf_op jit(solution)/shard_map/scatter-add | solution.py:75
  665.2 9.6 %scatter_custom_fusion.15 = f32[64,128]{1,0:T(8,128)S(1)} fusion(f32[64,128]{1,0:T(8,128)S(1)} %scatter_custom_fusion.14, s32[1536]{0:T(1024)S(1)} %fusion.137, f32[1536,128]{1,0:T(8,128)S(1)} %copy-done.1, f32[1536]{0:T(1024)S(1)} %mul.676), kind=kCustom, calls=%fused_computation.134 | custom fusion | flops 393216 | bytes 827392 | tf_op jit(solution)/shard_map/scatter-add | solution.py:75
  674.8 5.0 fusion.85
  698.6 9.3 %all-to-all-start = ((f32[32,1,512]{2,1,0:T(1,128)}), f32[32,1,512]{2,1,0:T(1,128)S(1)}, u32[]{:S(2)}, u32[]{:S(2)}) async-start(f32[32,1,512]{2,1,0:T(1,128)} %reshape.909), calls=%async_computation | async-start | bytes 131072 | tf_op jit(solution)/shard_map/all_to_all | solution.py:169
  709.2 9.8 %all-to-all-done = f32[32,1,512]{2,1,0:T(1,128)S(1)} async-done(((f32[32,1,512]{2,1,0:T(1,128)}), f32[32,1,512]{2,1,0:T(1,128)S(1)}, u32[]{:S(2)}, u32[]{:S(2)}) %all-to-all-start) | async-done | bytes 65568 | tf_op jit(solution)/shard_map/all_to_all | solution.py:169
  721.7 5.3 fusion.84
  727.0 5.3 fusion.86
  732.8 5.1 fusion.50
  737.9 5.1 fusion.48
  (261 shorter events, 109.2 us)
Async XLA Ops:
  7.2 9.7 %copy-start.26 = (f32[16,1,4,256]{3,2,1,0:T(4,128)S(1)}, f32[16,1,4,256]{3,2,1,0:T(4,128)}, u32[]{:S(2)}) copy-start(f32[16,1,4,256]{3,2,1,0:T(4,128)} %param.13) | copy-start | bytes 196612
  7.2 512.6 %all-reduce.4.cloned.1.call-start = ((), (), s32[]{:S(2)}) async-start(), calls=%async_computation.1 | async-start | bytes 4718592 | tf_op jit(solution)/shard_map/psum | solution.py:153
  8.5 8.1 %copy-start.10 = (f32[192,8,1]{0,2,1:T(1,128)}, f32[192,8,1]{0,2,1:T(1,128)S(1)}, u32[]{:S(2)}) copy-start(f32[192,8,1]{0,2,1:T(1,128)S(1)} %get-tuple-element.210) | copy-start | bytes 18436
  8.5 8.1 %copy-start.12 = (f32[192,8,1]{0,2,1:T(1,128)}, f32[192,8,1]{0,2,1:T(1,128)S(1)}, u32[]{:S(2)}) copy-start(f32[192,8,1]{0,2,1:T(1,128)S(1)} %get-tuple-element.204) | copy-start | bytes 18436
  8.5 8.1 %copy-start.14 = (f32[192,8,1]{0,2,1:T(1,128)}, f32[192,8,1]{0,2,1:T(1,128)S(1)}, u32[]{:S(2)}) copy-start(f32[192,8,1]{0,2,1:T(1,128)S(1)} %get-tuple-element.205) | copy-start | bytes 18436
  8.5 8.1 %copy-start.16 = (f32[192,8,1]{0,2,1:T(1,128)}, f32[192,8,1]{0,2,1:T(1,128)S(1)}, u32[]{:S(2)}) copy-start(f32[192,8,1]{0,2,1:T(1,128)S(1)} %get-tuple-element.206) | copy-start | bytes 18436
  8.6 8.1 %copy-start.18 = (f32[192,8,1]{0,2,1:T(1,128)}, f32[192,8,1]{0,2,1:T(1,128)S(1)}, u32[]{:S(2)}) copy-start(f32[192,8,1]{0,2,1:T(1,128)S(1)} %get-tuple-element.207) | copy-start | bytes 18436
  8.6 8.1 %copy-start.20 = (f32[192,8,1]{0,2,1:T(1,128)}, f32[192,8,1]{0,2,1:T(1,128)S(1)}, u32[]{:S(2)}) copy-start(f32[192,8,1]{0,2,1:T(1,128)S(1)} %get-tuple-element.208) | copy-start | bytes 18436
  8.6 8.1 %copy-start.22 = (f32[192,8,1]{0,2,1:T(1,128)}, f32[192,8,1]{0,2,1:T(1,128)S(1)}, u32[]{:S(2)}) copy-start(f32[192,8,1]{0,2,1:T(1,128)S(1)} %get-tuple-element.209) | copy-start | bytes 18436
  8.6 8.1 %copy-start.24 = (f32[192,8,1]{0,2,1:T(1,128)}, f32[192,8,1]{0,2,1:T(1,128)S(1)}, u32[]{:S(2)}) copy-start(f32[192,8,1]{0,2,1:T(1,128)S(1)} %get-tuple-element.203) | copy-start | bytes 18436
  9.6 7.1 copy-start.8
  49.3 4.7 copy-start.33
  49.3 4.9 copy-start.32
  49.3 5.0 copy-start.31
  49.3 5.2 copy-start.30
  49.3 5.3 copy-start.29
  49.3 5.5 copy-start.28
  49.3 5.6 copy-start.27
  181.5 18.1 %copy-start.35 = (s32[2,16]{1,0:T(2,128)}, s32[2,16]{1,0:T(2,128)S(1)}, u32[]{:S(2)}) copy-start(s32[2,16]{1,0:T(2,128)S(1)} %get-tuple-element.350) | copy-start | bytes 388 | tf_op jit(solution)/shard_map/while
  205.4 3.4 copy-start.2
  205.4 3.4 copy-start.7
  208.8 1.8 copy-start.36
  210.7 18.1 %copy-start.35 = (s32[2,16]{1,0:T(2,128)}, s32[2,16]{1,0:T(2,128)S(1)}, u32[]{:S(2)}) copy-start(s32[2,16]{1,0:T(2,128)S(1)} %get-tuple-element.350) | copy-start | bytes 388 | tf_op jit(solution)/shard_map/while
  234.6 3.9 copy-start.2
  234.6 3.9 copy-start.7
  238.4 1.8 copy-start.36
  240.3 2.6 copy-start.4
  244.0 1.7 copy-start.6
  244.0 1.7 copy-start.9
  519.8 10.4 %copy-start = (f32[1536,256]{1,0:T(8,128)S(1)}, f32[1536,256]{1,0:T(8,128)}, u32[]{:S(2)}) copy-start(f32[1536,256]{1,0:T(8,128)} %get-tuple-element.146) | copy-start | bytes 4718596
  578.8 19.3 %copy-start.1 = (f32[1536,128]{1,0:T(8,128)S(1)}, f32[1536,128]{1,0:T(8,128)}, u32[]{:S(2)}) copy-start(f32[1536,128]{1,0:T(8,128)} %get-tuple-element.145) | copy-start | bytes 2359300
  698.6 20.4 %all-to-all-start = ((f32[32,1,512]{2,1,0:T(1,128)}), f32[32,1,512]{2,1,0:T(1,128)S(1)}, u32[]{:S(2)}, u32[]{:S(2)}) async-start(f32[32,1,512]{2,1,0:T(1,128)} %reshape.909), calls=%async_computation | async-start | bytes 131072 | tf_op jit(solution)/shard_map/all_to_all | solution.py:169
  (12 other events, 12.1 us)
Sparse Core Ops, SparseCore 0:
  244.1 275.6 all-reduce.3
where the time goes:
time: 757 us; the launch traced here: 751 us
  waiting for transfers between devices  281 us (37%)
  other arithmetic  194 us (26%)
  blocking collectives  113 us (15%)
  local copies, waits for them, and re-layouts  78.8 us (10%)
  matrix products  59.3 us (8%)
  between operations  15.5 us (2%)
  starting transfers between devices  9.35 us (1%)
    psum x1, waiting for transfers between devices, on_device(): data_rows, weight_rows = lax.psum((data_rows, weight_rows), ('img', 'vol'))  271 us
    psum x1, blocking collectives, on_device(): slices = lax.psum(partial_value, ('img', 'vol')).astype(jnp.bfloat16)  113 us
    scatter-add x8, other arithmetic, spread_tiles(): acc_data = acc_data.at[target].add(scaled * data_rows, mode='drop')  78.1 us
    scatter-add x8, other arithmetic, spread_tiles(): acc_weight = acc_weight.at[target].add(scaled * weight_rows, mode='drop')  76.7 us
    gather x8, local copies, waits for them, and re-layouts, on_device(): jnp.take(flat_tiles, jnp.where(owned[:, :, term_index], local_row[:, :, t...  35.3 us
    mul x2, other arithmetic, shifted_weighted(): moved_re = (real_part * cosine - imag_part * sine) * factor  17.4 us
  transfers between devices with their start and end apart: 2, of which 2 were waited for; matrix products, arithmetic and copies ran while one was open for 1% of the time, Pallas kernels for 0%

commit v1 on v0

--- a/solution.py
+++ b/solution.py
@@ -150,7 +150,7 @@
     (back_data, back_weight), evidence = lax.scan(one_block, start, inputs)
     data_rows = back_data.reshape(orients * rows_per, width)
     weight_rows = back_weight.reshape(orients * rows_per, tile_len)
-    data_rows, weight_rows = lax.psum((data_rows, weight_rows), ("img", "vol"))
+    data_rows, weight_rows = lax.psum(lax.psum((data_rows, weight_rows), "vol"), "img")
     acc_data, acc_weight = spread_tiles(
         data_rows, weight_rows, owned, local_row, interp, slab_depth * planes_dev * per_line
     )

time: 757 us -> 941 us (1.24)
  waiting for transfers between devices: 281 us -> 462 us
    psum x1 -> x2, waiting for transfers between devices: 271 us -> 452 us  [the longest x1 302 us: on_device(): lax.psum((data_rows, weight_rows), 'vol')]
  transfers between devices with their start and end apart: 2 -> 3, of which waited for: 2 -> 3; matrix products, arithmetic and copies ran while one was open for 1% -> 1% of each run, Pallas kernels for 0% -> 0%
where the time goes in v1:
time: 941 us; the launch traced here: 934 us
  waiting for transfers between devices  462 us (49%)
  other arithmetic  194 us (21%)
  blocking collectives  113 us (12%)
  local copies, waits for them, and re-layouts  78 us (8%)
  matrix products  58.8 us (6%)
  between operations  15.5 us (2%)
  starting transfers between devices  12.4 us (1%)
    psum x1, waiting for transfers between devices, on_device(): lax.psum((data_rows, weight_rows), 'vol')  302 us
    psum x1, waiting for transfers between devices, on_device(): lax.psum(lax.psum((data_rows, weight_rows), 'vol'), 'img')  151 us
    psum x1, blocking collectives, on_device(): slices = lax.psum(partial_value, ('img', 'vol')).astype(jnp.bfloat16)  113 us
    scatter-add x8, other arithmetic, spread_tiles(): acc_data = acc_data.at[target].add(scaled * data_rows, mode='drop')  78 us
    scatter-add x8, other arithmetic, spread_tiles(): acc_weight = acc_weight.at[target].add(scaled * weight_rows, mode='drop')  77.1 us
    gather x8, local copies, waits for them, and re-layouts, on_device(): jnp.take(flat_tiles, jnp.where(owned[:, :, term_index], local_row[:, :, t...  35.3 us
  transfers between devices with their start and end apart: 3, of which 3 were waited for; matrix products, arithmetic and copies ran while one was open for 1% of the time, Pallas kernels for 0%

profile of v1, /device:TPU:1, one launch (start us, length us, event | category | flops | bytes accessed | tf_op | source)
XLA Modules:
  0.0 934.1 jit_solution(2143403855856749229)
XLA Ops:
  29.7 4.7 gather_fusion.5
  39.5 4.7 gather_fusion.7
  49.3 4.7 gather_fusion.1
  55.9 10.9 %fusion.17 = f32[1536,256]{1,0:T(8,128)} fusion(f32[1536,256]{1,0:T(8,128)} %gather_fusion.7, f32[1536,256]{1,0:T(8,128)} %gather_fusion.6, f32[1536,256]{1,0:T(8,128)} %gather_fusion.5, f32[1536,256]{1,0:T(8,128)} %gather_fusion.4, f32[1536,256]{1,0:T(8,128)S(1)} %gather_fusion.3, f32[1536,256]{1,0:T(8,128)S(1)} %gather_fusion.2, ...), kind=kLoop, calls=%fused_computation.71 | loop fusion | flops 9043968 | bytes 14217216 | tf_op jit(solution)/shard_map/reshape | solution.py:120
  66.8 112.6 %all-reduce.9 = bf16[1536,256]{1,0:T(8,128)(2,1)S(1)} all-reduce(f32[1536,256]{1,0:T(8,128)} %fusion.17), channel_id=1, replica_groups=mesh['img'=16,'vol'=32] {'img','vol'}, use_global_device_ids=true, to_apply=%region_0.2 | all-reduce | flops 393216 | bytes 2359296 | tf_op jit(solution)/shard_map/psum | solution.py:121
  181.5 58.6 %while.15 = (s32[]{:T(128)}, f32[192,2048]{1,0:T(8,128)}, f32[192,1024]{1,0:T(8,128)}, f32[2,16]{1,0:T(2,128)}, s32[2,16]{1,0:T(2,128)S(1)}, /*index=5*/s32[2,16...) while((s32[]{:T(128)}, f32[192,2048]{1,0:T(8,128)}, ...), condition=%wide.region_5.7_spmd.clone, body=%wide.region_1.6_spmd.clone.sunk | while | flops 1044547712 | bytes 34849968 | solution.py:150
  184.3 8.7 subtract_multiply_fusion.2
  213.4 8.7 subtract_multiply_fusion.2
  244.1 301.6 %all-reduce.6.cloned.1.call-done = (f32[1536,128]{1,0:T(8,128)}, f32[1536,256]{1,0:T(8,128)}) async-done(((f32[1536,128]{1,0:T(8,128)}, f32[1536,256]{1,0:T(8,128)}), (f32[1536,128]{1,0:T(8,128)}, f32[1536,256]{1,0:T(8,128)})) %all-reduce.6.cloned.1.call-update) | async-done | bytes 2359312 | tf_op jit(solution)/shard_map/psum | solution.py:153
  549.8 150.8 %all-reduce.8.cloned.1.call-done = (f32[1536,128]{1,0:T(8,128)}, f32[1536,256]{1,0:T(8,128)}) async-done(((f32[1536,128]{1,0:T(8,128)}, f32[1536,256]{1,0:T(8,128)}), (f32[1536,128]{1,0:T(8,128)}, f32[1536,256]{1,0:T(8,128)})) %all-reduce.8.cloned.1.call-update) | async-done | bytes 2359312 | tf_op jit(solution)/shard_map/psum | solution.py:153
  700.6 10.2 %scatter_custom_fusion = f32[64,256]{1,0:T(8,128)S(1)} fusion(s32[1536]{0:T(1024)S(1)} %fusion.130, f32[1536,256]{1,0:T(8,128)} %get-tuple-element.148, f32[1536]{0:T(1024)S(1)} %mul.631, f32[]{:T(128)} %constant.215.clone.1), kind=kCustom, calls=%fused_computation.106 | custom fusion | flops 786432 | bytes 1646596 | tf_op jit(solution)/shard_map/scatter-add | solution.py:74
  710.8 9.6 %scatter_custom_fusion.1 = f32[64,256]{1,0:T(8,128)S(1)} fusion(f32[64,256]{1,0:T(8,128)S(1)} %scatter_custom_fusion, s32[1536]{0:T(1024)S(1)} %fusion.131, f32[1536,256]{1,0:T(8,128)S(1)} %copy-done, f32[1536]{0:T(1024)S(1)} %mul.658), kind=kCustom, calls=%fused_computation.104 | custom fusion | flops 786432 | bytes 1646592 | tf_op jit(solution)/shard_map/scatter-add | solution.py:74
  720.4 9.6 %scatter_custom_fusion.2 = f32[64,256]{1,0:T(8,128)S(1)} fusion(f32[64,256]{1,0:T(8,128)S(1)} %scatter_custom_fusion.1, s32[1536]{0:T(1024)S(1)} %fusion.132, f32[1536,256]{1,0:T(8,128)S(1)} %copy-done, f32[1536]{0:T(1024)S(1)} %mul.661), kind=kCustom, calls=%fused_computation.102 | custom fusion | flops 786432 | bytes 1646592 | tf_op jit(solution)/shard_map/scatter-add | solution.py:74
  730.0 10.0 %scatter_custom_fusion.3 = f32[64,256]{1,0:T(8,128)S(1)} fusion(f32[64,256]{1,0:T(8,128)S(1)} %scatter_custom_fusion.2, s32[1536]{0:T(1024)S(1)} %fusion.133, f32[1536,256]{1,0:T(8,128)S(1)} %copy-done, f32[1536]{0:T(1024)S(1)} %mul.664), kind=kCustom, calls=%fused_computation.100 | custom fusion | flops 786432 | bytes 1646592 | tf_op jit(solution)/shard_map/scatter-add | solution.py:74
  740.0 9.6 %scatter_custom_fusion.4 = f32[64,256]{1,0:T(8,128)S(1)} fusion(f32[64,256]{1,0:T(8,128)S(1)} %scatter_custom_fusion.3, s32[1536]{0:T(1024)S(1)} %fusion.134, f32[1536,256]{1,0:T(8,128)S(1)} %copy-done, f32[1536]{0:T(1024)S(1)} %mul.667), kind=kCustom, calls=%fused_computation.98 | custom fusion | flops 786432 | bytes 1646592 | tf_op jit(solution)/shard_map/scatter-add | solution.py:74
  749.6 9.6 %scatter_custom_fusion.5 = f32[64,256]{1,0:T(8,128)S(1)} fusion(f32[64,256]{1,0:T(8,128)S(1)} %scatter_custom_fusion.4, s32[1536]{0:T(1024)S(1)} %fusion.135, f32[1536,256]{1,0:T(8,128)S(1)} %copy-done, f32[1536]{0:T(1024)S(1)} %mul.670), kind=kCustom, calls=%fused_computation.96 | custom fusion | flops 786432 | bytes 1646592 | tf_op jit(solution)/shard_map/scatter-add | solution.py:74
  759.3 9.6 %scatter_custom_fusion.6 = f32[64,256]{1,0:T(8,128)S(1)} fusion(f32[64,256]{1,0:T(8,128)S(1)} %scatter_custom_fusion.5, s32[1536]{0:T(1024)S(1)} %fusion.136, f32[1536,256]{1,0:T(8,128)S(1)} %copy-done, f32[1536]{0:T(1024)S(1)} %mul.673), kind=kCustom, calls=%fused_computation.94 | custom fusion | flops 786432 | bytes 1646592 | tf_op jit(solution)/shard_map/scatter-add | solution.py:74
  768.9 9.8 %scatter_custom_fusion.7 = f32[64,256]{1,0:T(8,128)S(1)} fusion(f32[64,256]{1,0:T(8,128)S(1)} %scatter_custom_fusion.6, s32[1536]{0:T(1024)S(1)} %fusion.137, f32[1536,256]{1,0:T(8,128)S(1)} %copy-done, f32[1536]{0:T(1024)S(1)} %mul.676), kind=kCustom, calls=%fused_computation.92 | custom fusion | flops 786432 | bytes 1646592 | tf_op jit(solution)/shard_map/scatter-add | solution.py:74
  778.7 9.5 %scatter_custom_fusion.8 = f32[64,128]{1,0:T(8,128)S(1)} fusion(s32[1536]{0:T(1024)S(1)} %fusion.130, f32[1536,128]{1,0:T(8,128)S(1)} %copy-done.1, f32[1536]{0:T(1024)S(1)} %mul.631, f32[]{:T(128)} %constant.229.clone.1), kind=kCustom, calls=%fused_computation.148 | custom fusion | flops 393216 | bytes 827396 | tf_op jit(solution)/shard_map/scatter-add | solution.py:75
  788.3 9.6 %scatter_custom_fusion.9 = f32[64,128]{1,0:T(8,128)S(1)} fusion(f32[64,128]{1,0:T(8,128)S(1)} %scatter_custom_fusion.8, s32[1536]{0:T(1024)S(1)} %fusion.131, f32[1536,128]{1,0:T(8,128)S(1)} %copy-done.1, f32[1536]{0:T(1024)S(1)} %mul.658), kind=kCustom, calls=%fused_computation.146 | custom fusion | flops 393216 | bytes 827392 | tf_op jit(solution)/shard_map/scatter-add | solution.py:75
  797.8 9.6 %scatter_custom_fusion.10 = f32[64,128]{1,0:T(8,128)S(1)} fusion(f32[64,128]{1,0:T(8,128)S(1)} %scatter_custom_fusion.9, s32[1536]{0:T(1024)S(1)} %fusion.132, f32[1536,128]{1,0:T(8,128)S(1)} %copy-done.1, f32[1536]{0:T(1024)S(1)} %mul.661), kind=kCustom, calls=%fused_computation.144 | custom fusion | flops 393216 | bytes 827392 | tf_op jit(solution)/shard_map/scatter-add | solution.py:75
  807.4 9.6 %scatter_custom_fusion.11 = f32[64,128]{1,0:T(8,128)S(1)} fusion(f32[64,128]{1,0:T(8,128)S(1)} %scatter_custom_fusion.10, s32[1536]{0:T(1024)S(1)} %fusion.133, f32[1536,128]{1,0:T(8,128)S(1)} %copy-done.1, f32[1536]{0:T(1024)S(1)} %mul.664), kind=kCustom, calls=%fused_computation.142 | custom fusion | flops 393216 | bytes 827392 | tf_op jit(solution)/shard_map/scatter-add | solution.py:75
  817.0 9.8 %scatter_custom_fusion.12 = f32[64,128]{1,0:T(8,128)S(1)} fusion(f32[64,128]{1,0:T(8,128)S(1)} %scatter_custom_fusion.11, s32[1536]{0:T(1024)S(1)} %fusion.134, f32[1536,128]{1,0:T(8,128)S(1)} %copy-done.1, f32[1536]{0:T(1024)S(1)} %mul.667), kind=kCustom, calls=%fused_computation.140 | custom fusion | flops 393216 | bytes 827392 | tf_op jit(solution)/shard_map/scatter-add | solution.py:75
  826.8 9.6 %scatter_custom_fusion.13 = f32[64,128]{1,0:T(8,128)S(1)} fusion(f32[64,128]{1,0:T(8,128)S(1)} %scatter_custom_fusion.12, s32[1536]{0:T(1024)S(1)} %fusion.135, f32[1536,128]{1,0:T(8,128)S(1)} %copy-done.1, f32[1536]{0:T(1024)S(1)} %mul.670), kind=kCustom, calls=%fused_computation.138 | custom fusion | flops 393216 | bytes 827392 | tf_op jit(solution)/shard_map/scatter-add | solution.py:75
  836.4 9.6 %scatter_custom_fusion.14 = f32[64,128]{1,0:T(8,128)S(1)} fusion(f32[64,128]{1,0:T(8,128)S(1)} %scatter_custom_fusion.13, s32[1536]{0:T(1024)S(1)} %fusion.136, f32[1536,128]{1,0:T(8,128)S(1)} %copy-done.1, f32[1536]{0:T(1024)S(1)} %mul.673), kind=kCustom, calls=%fused_computation.136 | custom fusion | flops 393216 | bytes 827392 | tf_op jit(solution)/shard_map/scatter-add | solution.py:75
  845.9 10.0 %scatter_custom_fusion.15 = f32[64,128]{1,0:T(8,128)S(1)} fusion(f32[64,128]{1,0:T(8,128)S(1)} %scatter_custom_fusion.14, s32[1536]{0:T(1024)S(1)} %fusion.137, f32[1536,128]{1,0:T(8,128)S(1)} %copy-done.1, f32[1536]{0:T(1024)S(1)} %mul.676), kind=kCustom, calls=%fused_computation.134 | custom fusion | flops 393216 | bytes 827392 | tf_op jit(solution)/shard_map/scatter-add | solution.py:75
  879.3 12.1 %all-to-all-start = ((f32[32,1,512]{2,1,0:T(1,128)}), f32[32,1,512]{2,1,0:T(1,128)S(1)}, u32[]{:S(2)}, u32[]{:S(2)}) async-start(f32[32,1,512]{2,1,0:T(1,128)} %reshape.909), calls=%async_computation | async-start | bytes 131072 | tf_op jit(solution)/shard_map/all_to_all | solution.py:169
  892.7 9.8 %all-to-all-done = f32[32,1,512]{2,1,0:T(1,128)S(1)} async-done(((f32[32,1,512]{2,1,0:T(1,128)}), f32[32,1,512]{2,1,0:T(1,128)S(1)}, u32[]{:S(2)}, u32[]{:S(2)}) %all-to-all-start) | async-done | bytes 65568 | tf_op jit(solution)/shard_map/all_to_all | solution.py:169
  905.2 5.3 fusion.84
  910.5 5.3 fusion.86
  916.3 5.1 fusion.50
  921.4 5.1 fusion.48
  (264 shorter events, 113.3 us)
Async XLA Ops:
  7.2 9.7 %copy-start.26 = (f32[16,1,4,256]{3,2,1,0:T(4,128)S(1)}, f32[16,1,4,256]{3,2,1,0:T(4,128)}, u32[]{:S(2)}) copy-start(f32[16,1,4,256]{3,2,1,0:T(4,128)} %param.13) | copy-start | bytes 196612
  7.2 538.6 %all-reduce.6.cloned.1.call-start = ((), (), s32[]{:S(2)}) async-start(), calls=%async_computation.1 | async-start | bytes 4718592 | tf_op jit(solution)/shard_map/psum | solution.py:153
  8.5 8.1 copy-start.10
  8.5 8.1 copy-start.12
  8.5 8.1 copy-start.14
  8.5 8.1 copy-start.16
  8.6 8.1 copy-start.18
  8.6 8.1 copy-start.20
  8.6 8.1 copy-start.22
  8.6 8.1 copy-start.24
  9.6 7.1 copy-start.8
  49.3 4.7 copy-start.33
  49.3 4.9 copy-start.32
  49.3 5.0 copy-start.31
  49.3 5.2 copy-start.30
  49.3 5.3 copy-start.29
  49.3 5.5 copy-start.28
  49.3 5.6 copy-start.27
  181.5 18.1 %copy-start.35 = (s32[2,16]{1,0:T(2,128)}, s32[2,16]{1,0:T(2,128)S(1)}, u32[]{:S(2)}) copy-start(s32[2,16]{1,0:T(2,128)S(1)} %get-tuple-element.352) | copy-start | bytes 388 | tf_op jit(solution)/shard_map/while
  210.6 18.1 %copy-start.35 = (s32[2,16]{1,0:T(2,128)}, s32[2,16]{1,0:T(2,128)S(1)}, u32[]{:S(2)}) copy-start(s32[2,16]{1,0:T(2,128)S(1)} %get-tuple-element.352) | copy-start | bytes 388 | tf_op jit(solution)/shard_map/while
  243.8 302.0 %copy-start.25 = (f32[192,8,1]{0,2,1:T(1,128)S(1)}, f32[192,8,1]{0,2,1:T(1,128)}, u32[]{:S(2)}) copy-start(f32[192,8,1]{0,2,1:T(1,128)} %copy-done.24) | copy-start | bytes 18436
  243.8 302.1 %copy-start.23 = (f32[192,8,1]{0,2,1:T(1,128)S(1)}, f32[192,8,1]{0,2,1:T(1,128)}, u32[]{:S(2)}) copy-start(f32[192,8,1]{0,2,1:T(1,128)} %copy-done.22) | copy-start | bytes 18436
  243.8 302.2 %copy-start.21 = (f32[192,8,1]{0,2,1:T(1,128)S(1)}, f32[192,8,1]{0,2,1:T(1,128)}, u32[]{:S(2)}) copy-start(f32[192,8,1]{0,2,1:T(1,128)} %copy-done.20) | copy-start | bytes 18436
  243.8 302.3 %copy-start.19 = (f32[192,8,1]{0,2,1:T(1,128)S(1)}, f32[192,8,1]{0,2,1:T(1,128)}, u32[]{:S(2)}) copy-start(f32[192,8,1]{0,2,1:T(1,128)} %copy-done.18) | copy-start | bytes 18436
  243.8 302.5 %copy-start.17 = (f32[192,8,1]{0,2,1:T(1,128)S(1)}, f32[192,8,1]{0,2,1:T(1,128)}, u32[]{:S(2)}) copy-start(f32[192,8,1]{0,2,1:T(1,128)} %copy-done.16) | copy-start | bytes 18436
  243.8 302.6 %copy-start.15 = (f32[192,8,1]{0,2,1:T(1,128)S(1)}, f32[192,8,1]{0,2,1:T(1,128)}, u32[]{:S(2)}) copy-start(f32[192,8,1]{0,2,1:T(1,128)} %copy-done.14) | copy-start | bytes 18436
  243.8 302.7 %copy-start.13 = (f32[192,8,1]{0,2,1:T(1,128)S(1)}, f32[192,8,1]{0,2,1:T(1,128)}, u32[]{:S(2)}) copy-start(f32[192,8,1]{0,2,1:T(1,128)} %copy-done.12) | copy-start | bytes 18436
  243.8 302.8 %copy-start.11 = (f32[192,8,1]{0,2,1:T(1,128)S(1)}, f32[192,8,1]{0,2,1:T(1,128)}, u32[]{:S(2)}) copy-start(f32[192,8,1]{0,2,1:T(1,128)} %copy-done.10) | copy-start | bytes 18436
  243.8 456.7 %all-reduce.8.cloned.1.call-start = ((), (), s32[]{:S(2)}) async-start(), calls=%async_computation.2 | async-start | bytes 4718592 | tf_op jit(solution)/shard_map/psum | solution.py:153
  700.6 10.2 %copy-start = (f32[1536,256]{1,0:T(8,128)S(1)}, f32[1536,256]{1,0:T(8,128)}, u32[]{:S(2)}) copy-start(f32[1536,256]{1,0:T(8,128)} %get-tuple-element.148) | copy-start | bytes 4718596
  759.3 19.5 %copy-start.1 = (f32[1536,128]{1,0:T(8,128)S(1)}, f32[1536,128]{1,0:T(8,128)}, u32[]{:S(2)}) copy-start(f32[1536,128]{1,0:T(8,128)} %get-tuple-element.147) | copy-start | bytes 2359300
  879.3 23.2 %all-to-all-start = ((f32[32,1,512]{2,1,0:T(1,128)}), f32[32,1,512]{2,1,0:T(1,128)S(1)}, u32[]{:S(2)}, u32[]{:S(2)}) async-start(f32[32,1,512]{2,1,0:T(1,128)} %reshape.909), calls=%async_computation | async-start | bytes 131072 | tf_op jit(solution)/shard_map/all_to_all | solution.py:169
  (13 other events, 26.2 us)
Sparse Core Ops, SparseCore 0:
  243.9 301.7 all-reduce.5
  548.7 151.8 all-reduce.7
